TPU v7x, 32 devices: a whole 2x2x4 slice. The times are simulated.
32 devices in a mesh: pb: 4 (over z), row: 4 (over y, x), col: 2 (over core).
Axes of the slice: x: 2, y: 2, z: 4, core: 2. Of those that a mesh axis runs over, the one named last changes fastest.
Arguments:
- amplitudes: bfloat16 [4, 20, 4, 9216], P('pb'), may hold values from -6 to 6
- pairs: int32 [4, 4, 2], P('pb'), may hold values from 0 to 3
- stored_k: int32 [4], replicated, may hold values from 0 to 3, each once
- orbitals: bfloat16 [4, 192, 2048], P('pb', None, ('row', 'col')), may hold values from -1.078125 to 1.078125
- valence_energy: float32 [4, 96], replicated, may hold values from -1 to 0
- conduction_energy: float32 [4, 96], replicated, may hold values from 2.5 to 3.5
- screened: bfloat16 [4, 2048, 2048], P('pb', 'row', 'col'), may hold values from -0.125 to 0.125
Outputs:
- filtered: bfloat16 [4, 20, 4, 9216], P('pb')
Inputs may be any that keep to these rules, and one draw needn't show every extreme that they name: stored_k holds every k-point exactly once; row s of orbitals belongs to k-point stored_k[s]. `pairs`: each entry is a k-point.
All inputs are finite; a program needn't handle non-finite values.
Results may differ from a plain program's by a relative error of at most 0.024.
Values may be sent and summed in bfloat16 or wider, within the bound.
A program may use at most 64 MiB of HBM per device.

v0:
```python
import jax
import jax.numpy as jnp
from jax import lax
from jax.sharding import PartitionSpec as P

CENTER = 3.0
HALF = 2.5


def on_device(amplitudes, pairs, stored_k, orbitals, valence_energy, conduction_energy, screened):
    amplitude = amplitudes[0]
    pair_list = pairs[0]
    w_tile = screened[0]
    count_v = valence_energy.shape[1]
    count_c = conduction_energy.shape[1]
    vectors, pair_count, flat_size = amplitude.shape
    points = orbitals.shape[2]
    col_width = w_tile.shape[1]
    column = lax.axis_index("col")

    def pick(shard_piece):
        pick_low = (stored_k[None, :] == pair_list[:, 0:1]).astype(jnp.bfloat16)
        pick_high = (stored_k[None, :] == pair_list[:, 1:2]).astype(jnp.bfloat16)
        low_bands = jnp.einsum(
            "pl,lbr->pbr", pick_low, shard_piece[:, :count_v], preferred_element_type=jnp.float32
        )
        high_bands = jnp.einsum(
            "pl,lbr->pbr", pick_high, shard_piece[:, count_v:], preferred_element_type=jnp.float32
        )
        return (low_bands, high_bands)

    def fetch_each():
        found = pick(lax.all_gather(orbitals, "pb", axis=0, tiled=True))
        return (found[0].astype(jnp.bfloat16), found[1].astype(jnp.bfloat16))

    low_energy = jnp.take(valence_energy, pair_list[:, 0], axis=0)
    high_energy = jnp.take(conduction_energy, pair_list[:, 1], axis=0)
    gap_grid = (high_energy[:, None, :] - low_energy[:, :, None]).reshape(pair_count, flat_size)
    gap_rows = jnp.tile(gap_grid, (vectors, 1))

    def kernel_term(current, bands):
        valence, conduction_orbital = bands
        amplitude_lattice = current.reshape(vectors, pair_count, count_v, count_c)
        inner_total_sum = jnp.einsum(
            "iomx,oxj->iomj",
            amplitude_lattice,
            conduction_orbital,
            preferred_element_type=jnp.float32,
        )
        values = jnp.sum(valence.astype(jnp.float32)[None] * inner_total_sum, axis=2)
        values = values.astype(jnp.bfloat16).reshape(vectors * pair_count, points)
        everywhere = lax.all_gather(values, ("row", "col"), axis=1, tiled=True)
        needed = lax.dynamic_slice_in_dim(everywhere, column * col_width, col_width, 1)
        partial_value = lax.dot_general(
            needed, w_tile, (((1,), (1,)), ((), ())), preferred_element_type=jnp.float32
        )
        own_sums = (
            lax.psum_scatter(
                partial_value.astype(jnp.bfloat16), "col", scatter_dimension=1, tiled=True
            )
            .astype(jnp.float32)
            .reshape(vectors, pair_count, points)
        )
        weighted_product = (valence.astype(jnp.float32)[None] * own_sums[:, :, None, :]).astype(
            jnp.bfloat16
        )
        projected = jnp.einsum(
            "kyqz,yhz->kyqh",
            weighted_product,
            conduction_orbital,
            preferred_element_type=jnp.float32,
        )
        return projected.reshape(vectors * pair_count, flat_size)

    def advance(current_rows, summed, gap_part, previous_rows, factor):
        value = (gap_part * current_rows + summed - CENTER * current_rows) / HALF
        if previous_rows is None:
            return value.astype(jnp.bfloat16)
        return (factor * value - previous_rows).astype(jnp.bfloat16)

    def finish(partial_term, current, previous, factor):
        summed = lax.psum(partial_term.astype(jnp.bfloat16), ("row", "col")).astype(jnp.float32)
        previous_full = None
        if previous is not None:
            previous_full = previous.astype(jnp.float32)
        return advance(current.astype(jnp.float32), summed, gap_rows, previous_full, factor)

    initial = amplitude.reshape(vectors * pair_count, flat_size)
    first_bands = fetch_each()
    first_term = finish(kernel_term(initial, first_bands), initial, None, 1.0)
    second_bands = fetch_each()
    second_term = finish(kernel_term(first_term, second_bands), first_term, initial, 2.0)
    return second_term.reshape(1, vectors, pair_count, flat_size)


def solution(mesh):
    return jax.shard_map(
        on_device,
        mesh=mesh,
        in_specs=(
            P("pb", None, None, None),
            P("pb", None, None),
            P(),
            P("pb", None, ("row", "col")),
            P(),
            P(),
            P("pb", "row", "col"),
        ),
        out_specs=P("pb", None, None, None),
        check_vma=False,
    )
```

profile of v0, /device:TPU:0, one launch (start us, length us, event | category | flops | bytes accessed | tf_op | source)
XLA Modules:
  0.0 231.6 jit_solution(977043757335007725)
XLA Ops:
  7.4 16.6 %all_gather.10 = bf16[4,192,256]{2,1,0:T(8,128)(2,1)S(1)} all-gather(bf16[1,192,256]{2,1,0:T(8,128)(2,1)} %param.12), channel_id=1, replica_groups=mesh['pb'=4,'row'=4,'col'=2] {'pb'}, dimensions={0}, use_global_device_ids=true | all-gather | bytes 491520 | tf_op jit(solution)/shard_map/all_gather | solution.py:33
  25.1 2.6 %reshape_reshape_squeeze.3 = bf16[20,4,96,96]{3,2,1,0:T(8,128)(2,1)} reshape(bf16[1,20,4,9216]{3,2,1,0:T(4,128)(2,1)S(1)} %copy-done.1) | data formatting | bytes 2949120 | tf_op jit(solution)/shard_map/reshape;reshape;squeeze | solution.py:43
  28.0 2.8 %fusion.1 = bf16[20,4,256]{2,0,1:T(8,128)(2,1)S(1)} fusion(f32[4,96,256]{2,1,0:T(8,128)S(1)} %copy.59, bf16[20,4,96,96]{3,2,1,0:T(8,128)(2,1)} %reshape_reshape_squeeze.3, bf16[4,96,256,1]{2,0,1,3:T(4,128)(2,1)S(1)} %fusion.16), kind=kOutput, calls=%fused_computation.5 | convolution fusion | flops 381399040 | bytes 2105344 | tf_op jit(solution)/shard_map/iomx,oxj->iomj/dot_general | solution.py:44
  30.9 10.1 %all_gather.11 = bf16[80,2048]{1,0:T(8,128)(2,1)S(1)} all-gather(bf16[80,256]{1,0:T(8,128)(2,1)S(1)} %convert_element_type.92), channel_id=1, replica_groups=mesh['pb'=4,'row'=4,'col'=2] {'row','col'}, dimensions={1}, use_global_device_ids=true | all-gather | bytes 368640 | tf_op jit(solution)/shard_map/all_gather | solution.py:52
  41.0 1.1 convolution_convert_fusion.3
  42.2 1.7 reshape.48
  43.9 6.7 %reduce-scatter.3.cloned.1.call-done = bf16[80,256]{1,0:T(8,128)(2,1)} async-done(((bf16[80,512]{1,0:T(8,128)(2,1)}), bf16[80,256]{1,0:T(8,128)(2,1)}) %reduce-scatter.3.cloned.1.call-update) | async-done | bytes 40976 | tf_op jit(solution)/shard_map/reduce_scatter | solution.py:58
  51.4 2.9 %convert_bitcast_fusion.1 = bf16[20,4,96,96]{2,3,0,1:T(8,128)(2,1)} fusion(f32[20,4,256]{2,0,1:T(8,128)S(1)} %copy.63, f32[4,96,256]{2,1,0:T(8,128)S(1)} %copy.59, bf16[4,96,256,1]{2,0,1,3:T(4,128)(2,1)S(1)} %copy-done.7), kind=kOutput, calls=%fused_computation.25 | convolution fusion | flops 382156800 | bytes 2146304 | tf_op jit(solution)/shard_map/kyqz,yhz->kyqh/dot_general | solution.py:67
  54.3 3.2 %copy.65 = bf16[20,4,96,96]{3,2,1,0:T(8,128)(2,1)S(1)} copy(bf16[20,4,96,96]{2,3,0,1:T(8,128)(2,1)} %convert_bitcast_fusion.1) | data formatting | bytes 2949120 | tf_op jit(solution)/shard_map/convert_element_type | solution.py:82
  57.6 3.6 %convert_element_type.97 = bf16[80,9216]{1,0:T(8,128)(2,1)} reshape(bf16[20,4,96,96]{3,2,1,0:T(8,128)(2,1)S(1)} %copy.65) | data formatting | bytes 2949120 | tf_op jit(solution)/shard_map/convert_element_type | solution.py:82
  62.8 2.3 tile.8
  65.0 4.3 %tile.9 = f32[80,9216]{1,0:T(8,128)} reshape(f32[20,4,9216]{2,1,0:T(4,128)} %tile.8) | data formatting | bytes 5898240 | tf_op jit(solution)/shard_map/tile | solution.py:39
  69.3 51.5 %all-reduce.3.cloned.1.call-done = bf16[80,9216]{1,0:T(8,128)(2,1)} async-done(((bf16[80,9216]{1,0:T(8,128)(2,1)}), bf16[80,9216]{1,0:T(8,128)(2,1)}) %all-reduce.3.cloned.1.call-update) | async-done | bytes 1474576 | tf_op jit(solution)/shard_map/psum | solution.py:82
  120.8 3.8 %multiply_convert_fusion.4 = bf16[80,9216]{1,0:T(8,128)(2,1)S(1)} fusion(f32[80,9216]{1,0:T(8,128)} %reshape.48, bf16[80,9216]{1,0:T(8,128)(2,1)} %all-reduce.3.cloned.1.call-done, f32[80,9216]{1,0:T(8,128)} %tile.9), kind=kLoop, calls=%fused_computation.21 | loop fusion | flops 5160960 | bytes 8847360 | tf_op jit(solution)/shard_map/convert_element_type | solution.py:78
  124.6 2.9 %reshape.46 = bf16[20,4,96,96]{3,2,1,0:T(8,128)(2,1)} reshape(bf16[80,9216]{1,0:T(8,128)(2,1)S(1)} %multiply_convert_fusion.4) | data formatting | bytes 2949120 | tf_op jit(solution)/shard_map/reshape | solution.py:43
  127.6 2.7 %fusion = bf16[20,4,256]{2,0,1:T(8,128)(2,1)S(1)} fusion(f32[4,96,256]{2,1,0:T(8,128)S(1)} %copy.59, bf16[20,4,96,96]{3,2,1,0:T(8,128)(2,1)} %reshape.46, bf16[4,96,256,1]{2,0,1,3:T(4,128)(2,1)S(1)} %copy-done.8), kind=kOutput, calls=%fused_computation.3 | convolution fusion | flops 381399040 | bytes 2105344 | tf_op jit(solution)/shard_map/iomx,oxj->iomj/dot_general | solution.py:44
  130.4 9.5 %all_gather.12 = bf16[80,2048]{1,0:T(8,128)(2,1)S(1)} all-gather(bf16[80,256]{1,0:T(8,128)(2,1)S(1)} %convert_element_type.102), channel_id=1, replica_groups=mesh['pb'=4,'row'=4,'col'=2] {'row','col'}, dimensions={1}, use_global_device_ids=true | all-gather | bytes 368640 | tf_op jit(solution)/shard_map/all_gather | solution.py:52
  141.2 7.4 %reduce-scatter.5.cloned.1.call-done = bf16[80,256]{1,0:T(8,128)(2,1)} async-done(((bf16[80,512]{1,0:T(8,128)(2,1)}), bf16[80,256]{1,0:T(8,128)(2,1)}) %reduce-scatter.5.cloned.1.call-update) | async-done | bytes 40976 | tf_op jit(solution)/shard_map/reduce_scatter | solution.py:58
  149.4 2.9 %convert_bitcast_fusion = bf16[20,4,96,96]{2,3,0,1:T(8,128)(2,1)} fusion(f32[20,4,256]{2,0,1:T(8,128)S(1)} %copy.69, f32[4,96,256]{2,1,0:T(8,128)S(1)} %copy.59, bf16[4,96,256,1]{2,0,1,3:T(4,128)(2,1)S(1)} %copy-done.8), kind=kOutput, calls=%fused_computation.24 | convolution fusion | flops 382156800 | bytes 2146304 | tf_op jit(solution)/shard_map/kyqz,yhz->kyqh/dot_general | solution.py:67
  152.3 3.2 %copy.71 = bf16[20,4,96,96]{3,2,1,0:T(8,128)(2,1)S(1)} copy(bf16[20,4,96,96]{2,3,0,1:T(8,128)(2,1)} %convert_bitcast_fusion) | data formatting | bytes 2949120 | tf_op jit(solution)/shard_map/convert_element_type | solution.py:82
  155.5 3.6 %convert_element_type.107 = bf16[80,9216]{1,0:T(8,128)(2,1)} reshape(bf16[20,4,96,96]{3,2,1,0:T(8,128)(2,1)S(1)} %copy.71) | data formatting | bytes 2949120 | tf_op jit(solution)/shard_map/convert_element_type | solution.py:82
  159.1 59.7 %all-reduce.5.cloned.1.call-done = bf16[80,9216]{1,0:T(8,128)(2,1)} async-done(((bf16[80,9216]{1,0:T(8,128)(2,1)}), bf16[80,9216]{1,0:T(8,128)(2,1)}) %all-reduce.5.cloned.1.call-update) | async-done | bytes 1474576 | tf_op jit(solution)/shard_map/psum | solution.py:82
  218.8 4.8 %fusion.12 = bf16[80,9216]{1,0:T(8,128)(2,1)S(1)} fusion(f32[80,9216]{1,0:T(8,128)} %reshape.48, f32[80,9216]{1,0:T(8,128)} %tile.9, bf16[80,9216]{1,0:T(8,128)(2,1)} %all-reduce.5.cloned.1.call-done, bf16[80,9216]{1,0:T(8,128)(2,1)} %all-reduce.3.cloned.1.call-done), kind=kLoop, calls=%fused_computation.20 | loop fusion | flops 11796480 | bytes 10321920 | tf_op jit(solution)/shard_map/convert_element_type | solution.py:79
  223.6 1.4 reshape.47
  (48 shorter events, 7.0 us)
Async XLA Ops:
  6.5 34.5 %copy-start = (bf16[1,512,1024]{2,1,0:T(8,128)(2,1)S(1)}, bf16[1,512,1024]{2,1,0:T(8,128)(2,1)}, u32[]{:S(2)}) copy-start(bf16[1,512,1024]{2,1,0:T(8,128)(2,1)} %param.15) | copy-start | bytes 3145732
  6.5 18.5 %copy-start.1 = (bf16[1,20,4,9216]{3,2,1,0:T(4,128)(2,1)S(1)}, bf16[1,20,4,9216]{3,2,1,0:T(4,128)(2,1)}, u32[]{:S(2)}) copy-start(bf16[1,20,4,9216]{3,2,1,0:T(4,128)(2,1)} %param.9) | copy-start | bytes 4423684
  6.5 44.1 %reduce-scatter.3.cloned.1.call-start = ((), (), s32[]{:S(2)}) async-start(), calls=%async_computation.2 | async-start | bytes 122880 | tf_op jit(solution)/shard_map/reduce_scatter | solution.py:58
  7.4 20.3 %copy-start.5 = (s32[4]{0:T(128)S(1)}, s32[4]{0:T(128)}, u32[]{:S(2)}) copy-start(s32[4]{0:T(128)} %param.11) | copy-start | bytes 52
  28.0 2.8 %copy-start.6 = (bf16[4,96,256,1]{2,0,1,3:T(4,128)(2,1)}, bf16[4,96,256,1]{2,0,1,3:T(4,128)(2,1)S(1)}, u32[]{:S(2)}) copy-start(bf16[4,96,256,1]{2,0,1,3:T(4,128)(2,1)S(1)} %fusion.16) | copy-start | bytes 589828
  41.0 2.9 %copy-start.4 = (s32[1,4,2]{1,2,0:T(2,128)S(1)}, s32[1,4,2]{1,2,0:T(2,128)}, u32[]{:S(2)}) copy-start(s32[1,4,2]{1,2,0:T(2,128)} %param.10) | copy-start | bytes 100
  42.1 9.3 %copy-start.7 = (bf16[4,96,256,1]{2,0,1,3:T(4,128)(2,1)S(1)}, bf16[4,96,256,1]{2,0,1,3:T(4,128)(2,1)}, u32[]{:S(2)}) copy-start(bf16[4,96,256,1]{2,0,1,3:T(4,128)(2,1)} %copy-done.6) | copy-start | bytes 589828
  42.1 78.7 %all-reduce.3.cloned.1.call-start = ((), (), s32[]{:S(2)}) async-start(), calls=%async_computation.3 | async-start | bytes 2949120 | tf_op jit(solution)/shard_map/psum | solution.py:82
  57.5 3.7 %copy-start.2 = (f32[4,96]{1,0:T(4,128)S(1)}, f32[4,96]{1,0:T(4,128)}, u32[]{:S(2)}) copy-start(f32[4,96]{1,0:T(4,128)} %param.13) | copy-start | bytes 4612
  57.5 4.2 %copy-start.3 = (f32[4,96]{1,0:T(4,128)S(1)}, f32[4,96]{1,0:T(4,128)}, u32[]{:S(2)}) copy-start(f32[4,96]{1,0:T(4,128)} %param.14) | copy-start | bytes 4612
  61.1 87.5 %reduce-scatter.5.cloned.1.call-start = ((), (), s32[]{:S(2)}) async-start(), calls=%async_computation.4 | async-start | bytes 122880 | tf_op jit(solution)/shard_map/reduce_scatter | solution.py:58
  124.6 2.9 %copy-start.8 = (bf16[4,96,256,1]{2,0,1,3:T(4,128)(2,1)S(1)}, bf16[4,96,256,1]{2,0,1,3:T(4,128)(2,1)}, u32[]{:S(2)}) copy-start(bf16[4,96,256,1]{2,0,1,3:T(4,128)(2,1)} %copy-done.6) | copy-start | bytes 589828
  140.9 77.9 %all-reduce.5.cloned.1.call-start = ((), (), s32[]{:S(2)}) async-start(), calls=%async_computation.5 | async-start | bytes 2949120 | tf_op jit(solution)/shard_map/psum | solution.py:82
Sparse Core Ops, SparseCore 0:
  42.2 8.3 reduce-scatter.2
  61.3 59.5 all-reduce.2
  141.1 7.5 reduce-scatter.4
  159.2 59.5 all-reduce.4
where the time goes:
time: 232 us
  waiting for transfers between devices  125 us (54%)
  blocking collectives  36.2 us (16%)
  local copies, waits for them, and re-layouts  32.7 us (14%)
  matrix products  14.8 us (6%)
  between operations  13.3 us (6%)
  other arithmetic  8.91 us (4%)
    psum x2, waiting for transfers between devices, finish(): lax.psum(partial_term.astype(jnp.bfloat16), ('row', 'col'))  111 us
    all_gather x2, blocking collectives, kernel_term(): everywhere = lax.all_gather(values, ('row', 'col'), axis=1, tiled=True)  19.6 us
    all_gather x1, blocking collectives, fetch_each(): found = pick(lax.all_gather(orbitals, 'pb', axis=0, tiled=True))  16.6 us
    reduce_scatter x2, waiting for transfers between devices, kernel_term(): lax.psum_scatter(partial_value.astype(jnp.bfloat16), 'col', scatter_dimen...  14.1 us
    convert_element_type x4, local copies, waits for them, and re-layouts, finish(): partial_term.astype(jnp.bfloat16)  13.5 us
    another operation x2, local copies, waits for them, and re-layouts, on_device(): gap_rows = jnp.tile(gap_grid, (vectors, 1))  6.56 us
    dot_general x2, matrix products, kernel_term(): jnp.einsum('kyqz,yhz->kyqh', weighted_product, conduction_orbital, prefer...  5.75 us
    dot_general x2, matrix products, kernel_term(): jnp.einsum('iomx,oxj->iomj', amplitude_lattice, conduction_orbital, prefe...  5.54 us
  transfers between devices with their start and end apart: 4, of which 4 were waited for; matrix products, arithmetic and copies ran while one was open for 4% of the time, Pallas kernels for 0%

commit v1 on v0

--- a/solution.py
+++ b/solution.py
@@ -79,7 +79,9 @@
         return (factor * value - previous_rows).astype(jnp.bfloat16)
 
     def finish(partial_term, current, previous, factor):
-        summed = lax.psum(partial_term.astype(jnp.bfloat16), ("row", "col")).astype(jnp.float32)
+        summed = jnp.sum(
+            lax.all_gather(partial_term.astype(jnp.bfloat16), ("row", "col")), axis=0
+        ).astype(jnp.float32)
         previous_full = None
         if previous is not None:
             previous_full = previous.astype(jnp.float32)

time: 232 us -> 268 us (1.16)
  waiting for transfers between devices: 125 us -> 152 us
  other arithmetic: 8.91 us -> 18.6 us
  local copies, waits for them, and re-layouts: 32.7 us -> 29.2 us
    all_gather x0 -> x2, waiting for transfers between devices: none -> 136 us  [finish(): lax.all_gather(partial_term.astype(jnp.bfloat16), ('row', 'col'))]
    psum x2 -> x0, waiting for transfers between devices: 111 us -> none  [finish(): lax.psum(partial_term.astype(jnp.bfloat16), ('row', 'col'))]
    reduce_sum x0 -> x2, other arithmetic: none -> 13 us  [finish(): jnp.sum(lax.all_gather(partial_term.astype(jnp.bfloat16), ('row', 'col'))...]
    another operation x2 -> x0, local copies, waits for them, and re-layouts: 6.56 us -> none  [on_device(): gap_rows = jnp.tile(gap_grid, (vectors, 1))]
    convert_element_type x1 -> x3, local copies, waits for them, and re-layouts: 1.73 us -> 7.25 us  [finish(): summed = jnp.sum(lax.all_gather(partial_term.astype(jnp.bfloat16), ('row'...]
    reshape x2 -> x0, local copies, waits for them, and re-layouts: 4.34 us -> none  [the longest x1 2.91 us: kernel_term(): amplitude_lattice = current.reshape(vectors, pair_count, count_v, count_c)]
    convert_element_type x1 -> x0, other arithmetic: 3.8 us -> none  [advance(): return value.astype(jnp.bfloat16)]
  transfers between devices with their start and end apart: 4 -> 4, of which waited for: 4 -> 4; matrix products, arithmetic and copies ran while one was open for 4% -> 1% of each run, Pallas kernels for 0% -> 0%
where the time goes in v1:
time: 268 us
  waiting for transfers between devices  152 us (57%)
  blocking collectives  37 us (14%)
  local copies, waits for them, and re-layouts  29.2 us (11%)
  other arithmetic  18.6 us (7%)
  matrix products  17.3 us (6%)
  between operations  13.3 us (5%)
    all_gather x2, waiting for transfers between devices, finish(): lax.all_gather(partial_term.astype(jnp.bfloat16), ('row', 'col'))  136 us
    all_gather x2, blocking collectives, kernel_term(): everywhere = lax.all_gather(values, ('row', 'col'), axis=1, tiled=True)  20.4 us
    all_gather x1, blocking collectives, fetch_each(): found = pick(lax.all_gather(orbitals, 'pb', axis=0, tiled=True))  16.6 us
    reduce_scatter x2, waiting for transfers between devices, kernel_term(): lax.psum_scatter(partial_value.astype(jnp.bfloat16), 'col', scatter_dimen...  16.1 us
    convert_element_type x4, local copies, waits for them, and re-layouts, finish(): partial_term.astype(jnp.bfloat16)  15.3 us
    reduce_sum x2, other arithmetic, finish(): jnp.sum(lax.all_gather(partial_term.astype(jnp.bfloat16), ('row', 'col'))...  13 us
    convert_element_type x3, local copies, waits for them, and re-layouts, finish(): summed = jnp.sum(lax.all_gather(partial_term.astype(jnp.bfloat16), ('row'...  7.25 us
    dot_general x2, matrix products, kernel_term(): jnp.einsum('iomx,oxj->iomj', amplitude_lattice, conduction_orbital, prefe...  7.13 us
  transfers between devices with their start and end apart: 4, of which 4 were waited for; matrix products, arithmetic and copies ran while one was open for 1% of the time, Pallas kernels for 0%

profile of v1, /device:TPU:0, one launch (start us, length us, event | category | flops | bytes accessed | tf_op | source)
XLA Modules:
  0.0 267.8 jit_solution(17216310436765954970)
XLA Ops:
  7.4 16.6 %all_gather.18 = bf16[4,192,256]{2,1,0:T(8,128)(2,1)S(1)} all-gather(bf16[1,192,256]{2,1,0:T(8,128)(2,1)} %param.12), channel_id=1, replica_groups=mesh['pb'=4,'row'=4,'col'=2] {'pb'}, dimensions={0}, use_global_device_ids=true | all-gather | bytes 491520 | tf_op jit(solution)/shard_map/all_gather | solution.py:33
  25.1 2.6 reshape_reshape_squeeze.3
  28.0 2.8 %fusion.1 = bf16[20,4,256]{2,0,1:T(8,128)(2,1)S(1)} fusion(f32[4,96,256]{2,1,0:T(8,128)S(1)} %copy.60, bf16[20,4,96,96]{3,2,1,0:T(8,128)(2,1)} %reshape_reshape_squeeze.3, bf16[4,96,256,1]{2,0,1,3:T(4,128)(2,1)S(1)} %fusion.23), kind=kOutput, calls=%fused_computation.5 | convolution fusion | flops 381399040 | bytes 2105344 | tf_op jit(solution)/shard_map/iomx,oxj->iomj/dot_general | solution.py:44
  30.9 10.1 %all_gather.19 = bf16[80,2048]{1,0:T(8,128)(2,1)S(1)} all-gather(bf16[80,256]{1,0:T(8,128)(2,1)S(1)} %convert_element_type.142), channel_id=1, replica_groups=mesh['pb'=4,'row'=4,'col'=2] {'row','col'}, dimensions={1}, use_global_device_ids=true | all-gather | bytes 368640 | tf_op jit(solution)/shard_map/all_gather | solution.py:52
  41.0 1.1 convolution_convert_fusion.3
  42.2 8.4 %reduce-scatter.3.cloned.1.call-done = bf16[80,256]{1,0:T(8,128)(2,1)} async-done(((bf16[80,512]{1,0:T(8,128)(2,1)}), bf16[80,256]{1,0:T(8,128)(2,1)}) %reduce-scatter.3.cloned.1.call-update) | async-done | bytes 40976 | tf_op jit(solution)/shard_map/reduce_scatter | solution.py:58
  51.4 2.9 %convert_bitcast_fusion.1 = bf16[20,4,96,96]{2,3,0,1:T(8,128)(2,1)} fusion(f32[20,4,256]{2,0,1:T(8,128)S(1)} %copy.64, f32[4,96,256]{2,1,0:T(8,128)S(1)} %copy.60, bf16[4,96,256,1]{2,0,1,3:T(4,128)(2,1)S(1)} %fusion.23), kind=kOutput, calls=%fused_computation.36 | convolution fusion | flops 382156800 | bytes 2146304 | tf_op jit(solution)/shard_map/kyqz,yhz->kyqh/dot_general | solution.py:67
  54.3 3.2 %copy.66 = bf16[20,4,96,96]{3,2,1,0:T(8,128)(2,1)S(1)} copy(bf16[20,4,96,96]{2,3,0,1:T(8,128)(2,1)} %convert_bitcast_fusion.1) | data formatting | bytes 2949120 | tf_op jit(solution)/shard_map/convert_element_type | solution.py:83
  57.6 3.6 %convert_element_type.147 = bf16[1,80,9216]{2,1,0:T(8,128)(2,1)} reshape(bf16[20,4,96,96]{3,2,1,0:T(8,128)(2,1)S(1)} %copy.66) | data formatting | bytes 2949120 | tf_op jit(solution)/shard_map/convert_element_type | solution.py:83
  62.7 68.5 %all-gather.3.cloned.1.call-done = bf16[8,80,9216]{2,1,0:T(8,128)(2,1)} async-done(((bf16[1,80,9216]{2,1,0:T(8,128)(2,1)}), bf16[8,80,9216]{2,1,0:T(8,128)(2,1)}) %all-gather.3.cloned.1.call-update) | async-done | bytes 11796496 | tf_op jit(solution)/shard_map/all_gather | solution.py:83
  131.2 6.5 %reduce_sum.43 = bf16[80,9216]{1,0:T(8,128)(2,1)S(1)} reduce(bf16[8,80,9216]{2,1,0:T(8,128)(2,1)} %all-gather.3.cloned.1.call-done, bf16[]{:T(256)} %constant.30.clone.1), dimensions={0}, to_apply=%region_2.4 | reduce | flops 5160960 | bytes 13271042 | tf_op jit(solution)/shard_map/reduce_sum | solution.py:82
  137.7 3.0 %reshape.93 = f32[20,4,96,96]{3,2,1,0:T(8,128)} reshape(bf16[80,9216]{1,0:T(8,128)(2,1)S(1)} %reduce_sum.43) | data formatting | bytes 4423680 | tf_op jit(solution)/shard_map/convert_element_type | solution.py:84
  140.7 4.3 %fusion = bf16[20,4,256]{2,0,1:T(8,128)(2,1)S(1)} fusion(f32[4,96,256]{2,1,0:T(8,128)S(1)} %copy.60, bf16[4,96,256,1]{2,0,1,3:T(4,128)(2,1)S(1)} %copy-done.7, f32[20,4,96,96]{3,2,1,0:T(8,128)} %reshape.93, bf16[20,4,96,96]{3,2,1,0:T(8,128)(2,1)} %reshape_reshape_squeeze.3, f32[4,96,96]{2,1,0:T(8,128)S(1)} %broadcast_subtract_fusion), kind=kOutput, calls=%fused_computation.3 | convolution fusion | flops 386560000 | bytes 5201920 | tf_op jit(solution)/shard_map/iomx,oxj->iomj/dot_general | solution.py:44
  145.1 10.2 %all_gather.21 = bf16[80,2048]{1,0:T(8,128)(2,1)S(1)} all-gather(bf16[80,256]{1,0:T(8,128)(2,1)S(1)} %convert_element_type.157), channel_id=1, replica_groups=mesh['pb'=4,'row'=4,'col'=2] {'row','col'}, dimensions={1}, use_global_device_ids=true | all-gather | bytes 368640 | tf_op jit(solution)/shard_map/all_gather | solution.py:52
  155.3 1.1 convolution_convert_fusion.2
  156.5 7.7 %reduce-scatter.5.cloned.1.call-done = bf16[80,256]{1,0:T(8,128)(2,1)} async-done(((bf16[80,512]{1,0:T(8,128)(2,1)}), bf16[80,256]{1,0:T(8,128)(2,1)}) %reduce-scatter.5.cloned.1.call-update) | async-done | bytes 40976 | tf_op jit(solution)/shard_map/reduce_scatter | solution.py:58
  165.0 3.8 %convert_bitcast_fusion = bf16[20,4,96,96]{2,3,0,1:T(8,128)(2,1)} fusion(f32[20,4,256]{2,0,1:T(8,128)S(1)} %copy.70, f32[4,96,256]{2,1,0:T(8,128)S(1)} %copy.60, bf16[4,96,256,1]{2,0,1,3:T(4,128)(2,1)} %copy-done.6), kind=kOutput, calls=%fused_computation.35 | convolution fusion | flops 382156800 | bytes 2146304 | tf_op jit(solution)/shard_map/kyqz,yhz->kyqh/dot_general | solution.py:67
  168.8 3.9 %copy.72 = bf16[20,4,96,96]{3,2,1,0:T(8,128)(2,1)} copy(bf16[20,4,96,96]{2,3,0,1:T(8,128)(2,1)} %convert_bitcast_fusion) | data formatting | bytes 2949120 | tf_op jit(solution)/shard_map/convert_element_type | solution.py:83
  172.7 4.6 %convert_element_type.162 = bf16[1,80,9216]{2,1,0:T(8,128)(2,1)} reshape(bf16[20,4,96,96]{3,2,1,0:T(8,128)(2,1)} %copy.72) | data formatting | bytes 2949120 | tf_op jit(solution)/shard_map/convert_element_type | solution.py:83
  177.6 2.1 reshape.92
  179.7 67.6 %all-gather.5.cloned.1.call-done = bf16[8,80,9216]{2,1,0:T(8,128)(2,1)} async-done(((bf16[1,80,9216]{2,1,0:T(8,128)(2,1)}), bf16[8,80,9216]{2,1,0:T(8,128)(2,1)}) %all-gather.5.cloned.1.call-update) | async-done | bytes 11796496 | tf_op jit(solution)/shard_map/all_gather | solution.py:83
  247.3 6.5 %reduce_sum.45 = bf16[80,9216]{1,0:T(8,128)(2,1)S(1)} reduce(bf16[8,80,9216]{2,1,0:T(8,128)(2,1)} %all-gather.5.cloned.1.call-done, bf16[]{:T(256)} %constant.30.clone.1), dimensions={0}, to_apply=%region_5.7 | reduce | flops 5160960 | bytes 13271042 | tf_op jit(solution)/shard_map/reduce_sum | solution.py:82
  253.8 2.1 reshape.95
  255.9 5.4 %fusion.19 = bf16[1,20,4,9216]{3,2,1,0:T(4,128)(2,1)} fusion(bf16[1,20,4,9216]{3,2,1,0:T(4,128)(2,1)} %param.9, f32[1,20,4,9216]{3,2,1,0:T(4,128)} %reshape.95, f32[1,20,4,9216]{3,2,1,0:T(4,128)} %reshape.92, f32[4,9216]{1,0:T(4,128)S(1)} %sub.39), kind=kLoop, calls=%fused_computation.32 | loop fusion | flops 11059200 | bytes 8994816 | tf_op jit(solution)/shard_map/convert_element_type | solution.py:79
  (45 shorter events, 5.8 us)
Async XLA Ops:
  6.5 34.5 %copy-start = (bf16[1,512,1024]{2,1,0:T(8,128)(2,1)S(1)}, bf16[1,512,1024]{2,1,0:T(8,128)(2,1)}, u32[]{:S(2)}) copy-start(bf16[1,512,1024]{2,1,0:T(8,128)(2,1)} %param.15) | copy-start | bytes 3145732
  6.5 18.5 %copy-start.1 = (bf16[1,20,4,9216]{3,2,1,0:T(4,128)(2,1)S(1)}, bf16[1,20,4,9216]{3,2,1,0:T(4,128)(2,1)}, u32[]{:S(2)}) copy-start(bf16[1,20,4,9216]{3,2,1,0:T(4,128)(2,1)} %param.9) | copy-start | bytes 4423684
  6.5 44.1 %reduce-scatter.3.cloned.1.call-start = ((), (), s32[]{:S(2)}) async-start(), calls=%async_computation.2 | async-start | bytes 122880 | tf_op jit(solution)/shard_map/reduce_scatter | solution.py:58
  7.4 20.3 %copy-start.5 = (s32[4]{0:T(128)S(1)}, s32[4]{0:T(128)}, u32[]{:S(2)}) copy-start(s32[4]{0:T(128)} %param.11) | copy-start | bytes 52
  28.0 23.4 %copy-start.6 = (bf16[4,96,256,1]{2,0,1,3:T(4,128)(2,1)}, bf16[4,96,256,1]{2,0,1,3:T(4,128)(2,1)S(1)}, u32[]{:S(2)}) copy-start(bf16[4,96,256,1]{2,0,1,3:T(4,128)(2,1)S(1)} %fusion.23) | copy-start | bytes 589828
  42.1 89.0 %all-gather.3.cloned.1.call-start = ((), (), s32[]{:S(2)}) async-start(), calls=%async_computation.3 | async-start | bytes 13271040 | tf_op jit(solution)/shard_map/all_gather | solution.py:83
  57.5 3.7 %copy-start.4 = (s32[1,4,2]{1,2,0:T(2,128)S(1)}, s32[1,4,2]{1,2,0:T(2,128)}, u32[]{:S(2)}) copy-start(s32[1,4,2]{1,2,0:T(2,128)} %param.10) | copy-start | bytes 100
  57.6 3.7 %copy-start.2 = (f32[4,96]{1,0:T(4,128)S(1)}, f32[4,96]{1,0:T(4,128)}, u32[]{:S(2)}) copy-start(f32[4,96]{1,0:T(4,128)} %param.13) | copy-start | bytes 4612
  57.6 4.3 %copy-start.3 = (f32[4,96]{1,0:T(4,128)S(1)}, f32[4,96]{1,0:T(4,128)}, u32[]{:S(2)}) copy-start(f32[4,96]{1,0:T(4,128)} %param.14) | copy-start | bytes 4612
  61.2 103.0 %reduce-scatter.5.cloned.1.call-start = ((), (), s32[]{:S(2)}) async-start(), calls=%async_computation.4 | async-start | bytes 122880 | tf_op jit(solution)/shard_map/reduce_scatter | solution.py:58
  137.6 3.0 %copy-start.7 = (bf16[4,96,256,1]{2,0,1,3:T(4,128)(2,1)S(1)}, bf16[4,96,256,1]{2,0,1,3:T(4,128)(2,1)}, u32[]{:S(2)}) copy-start(bf16[4,96,256,1]{2,0,1,3:T(4,128)(2,1)} %copy-done.6) | copy-start | bytes 589828
  156.4 90.9 %all-gather.5.cloned.1.call-start = ((), (), s32[]{:S(2)}) async-start(), calls=%async_computation.5 | async-start | bytes 13271040 | tf_op jit(solution)/shard_map/all_gather | solution.py:83
Sparse Core Ops, SparseCore 0:
  42.2 8.3 reduce-scatter.2
  61.3 69.8 all-gather.2
  156.5 7.5 reduce-scatter.4
  177.5 69.7 all-gather.4
